TPU v7x, 128 devices: a whole 4x4x4 slice. The times are simulated.
128 devices in a mesh: row: 8 (over y, core), col: 16 (over x, z).
Axes of the slice: x: 4, y: 4, z: 4, core: 2. Of those that a mesh axis runs over, the one named last changes fastest.
Arguments:
- contribution: float32 [8, 8, 4, 16, 128, 128], P(None, 'row', None, 'col'), may hold values from -6 to 6
- parent_tiles: float32 [16, 8, 8, 16, 128, 128], P(None, 'row', None, 'col'), may hold values from -6 to 6
- row_basis: float32 [8, 8, 64, 128], P(None, 'row'), may hold values from -2.4 to 2.4
- pivot_basis: float32 [8, 8, 64, 2048], P(None, 'row', None, 'col'), may hold values from -0.125 to 0.125
- tile_ranks: int32 [64], replicated, may hold values from 16 to 64, as said below
- block_map: int32 [64], replicated, may hold values from 0 to 127, as said below
- panel_start: int32 [1], replicated, may hold values from 0 to 63
- pivot_inverse: float32 [512, 512], replicated
Outputs:
- updated_parent: float32 [16, 8, 8, 16, 128, 128], P(None, 'row', None, 'col')
Inputs may be any that keep to these rules, and one draw needn't show every extreme that they name: `tile_ranks`: multiples of 16; both 16 and 64 occur. `block_map`: child tile row u * 16 + l, for 0 <= l < 16, maps to parent tile row 2 * 16 * u + h_u + l with 0 <= h_u < 16; the 4 values h_u are distinct modulo 8.
All inputs are finite; a program needn't handle non-finite values.
Results may differ from a plain program's by a relative error of at most 0.0003.
Values sent between devices are 32-bit elements; how exact they have to be, the bound alone decides.
No kernel may reach another device: no remote copies, remote signals or barrier semaphores. Data moves between devices by JAX's collectives and lax.ppermute only.
A program may use at most 128 MiB of HBM per device.

v0:
```python
import jax
import jax.numpy as jnp
from jax import lax
from jax.sharding import PartitionSpec as P

PANEL_T = 4
highest = lax.Precision.HIGHEST


def spread_2(x, axis, root):
    mine = lax.axis_index(axis) == root
    return lax.psum(jnp.where(mine, x, jnp.zeros_like(x)), axis)


def from_behind(x, axis, by):
    count = lax.axis_size(axis)
    return lax.ppermute(x, axis, [(i, (i + by) % count) for i in range(count)])


def select_entries(lookup, wanted):
    matches = wanted[:, None] == jnp.arange(lookup.shape[0], dtype=jnp.int32)[None, :]
    return jnp.sum(jnp.where(matches, lookup[None, :], 0), axis=1)


def keep_ranks(factor, tile_index, rank_table):
    limits = select_entries(rank_table, tile_index)
    kept_cols = (jnp.arange(factor.shape[1], dtype=jnp.int32)[None, :] < limits[:, None]).astype(
        jnp.float32
    )
    return factor * kept_cols[:, :, None]


def every_other(stacked, groups, offset):
    shaped = stacked.reshape((groups, stacked.shape[0] // groups) + stacked.shape[1:])
    return lax.dynamic_index_in_dim(shaped, offset, axis=1, keepdims=False)


def per_device(
    contribution,
    parent_tiles,
    row_basis,
    pivot_basis,
    tile_ranks,
    block_map,
    panel_start,
    pivot_inverse,
):
    rows_grid = lax.axis_size("row")
    cols_grid = lax.axis_size("col")
    my_row = lax.axis_index("row")
    my_col = lax.axis_index("col")
    local_rows = contribution.shape[0]
    local_cols = contribution.shape[2]
    parent_rows = parent_tiles.shape[0]
    parent_cols = parent_tiles.shape[2]
    rank_max = row_basis.shape[2]
    per_block = cols_grid // rows_grid
    row_index = jnp.arange(local_rows, dtype=jnp.int32) * rows_grid + my_row
    col_index = jnp.arange(local_cols, dtype=jnp.int32) * cols_grid + my_col
    root_row = my_col % rows_grid
    offset = my_col // rows_grid
    own_basis = keep_ranks(row_basis[:, 0], row_index, tile_ranks)
    own_pivots = pivot_basis[:, 0]
    basis_picked = every_other(row_basis[:, 0], local_cols, offset)
    col_basis = spread_2(basis_picked, "row", root_row)
    all_pivots = lax.all_gather(pivot_basis, "row", axis=1, tiled=True)
    pivot_width = pivot_basis.shape[3]
    grouped = all_pivots.reshape(local_cols, cols_grid, rank_max, pivot_width)
    products = jnp.einsum(
        "trp,scup->cstru",
        own_pivots,
        grouped,
        precision=highest,
        preferred_element_type=jnp.float32,
    )
    weights = lax.psum_scatter(
        products.reshape(lax.axis_size("col") * local_cols, local_rows, rank_max * rank_max),
        "col",
        scatter_dimension=0,
        tiled=True,
    )
    weights = weights.reshape(local_cols, local_rows, rank_max, rank_max)
    col_basis = keep_ranks(col_basis, col_index, tile_ranks)
    half_product = jnp.einsum(
        "trx,stru->tsux", own_basis, weights, precision=highest, preferred_element_type=jnp.float32
    )
    update = jnp.einsum(
        "tsux,suy->tsxy",
        half_product,
        col_basis,
        precision=highest,
        preferred_element_type=jnp.float32,
    )
    lower_mask = (row_index[:, None] >= col_index[None, :])[:, :, None, None]
    payload = jnp.where(lower_mask, contribution[:, 0, :, 0] - update, jnp.float32(0.0))
    block_first = jnp.arange(local_cols, dtype=jnp.int32) * cols_grid
    shifts = select_entries(block_map, block_first) - 2 * block_first
    row_shift = jnp.repeat(shifts, per_block) % rows_grid
    for bit_index in range((rows_grid - 1).bit_length()):
        arrived = from_behind(payload, "row", 1 << bit_index)
        taken = row_shift // (1 << bit_index) % 2 == 1
        payload = jnp.where(taken[:, None, None, None], arrived, payload)
    for bit_index in range((cols_grid - 1).bit_length()):
        arrived = from_behind(payload, "col", 1 << bit_index)
        taken = shifts // (1 << bit_index) % 2 == 1
        payload = jnp.where(taken[None, :, None, None], arrived, payload)
    row_source = (my_row - row_shift) % rows_grid
    target_rows = (
        select_entries(block_map, jnp.arange(local_rows, dtype=jnp.int32) * rows_grid + row_source)
        // rows_grid
    )
    col_source = (my_col - shifts) % cols_grid
    target_cols = (
        select_entries(block_map, jnp.arange(local_cols, dtype=jnp.int32) * cols_grid + col_source)
        // cols_grid
    )
    row_place = (jnp.arange(parent_rows, dtype=jnp.int32)[:, None] == target_rows[None, :]).astype(
        jnp.float32
    )
    col_place = (jnp.arange(parent_cols, dtype=jnp.int32)[:, None] == target_cols[None, :]).astype(
        jnp.float32
    )
    spread = jnp.einsum(
        "at,tsxy->asxy", row_place, payload, precision=highest, preferred_element_type=jnp.float32
    )
    spread = jnp.einsum(
        "bs,asxy->abxy", col_place, spread, precision=highest, preferred_element_type=jnp.float32
    )
    assembled = parent_tiles[:, 0, :, 0] + spread
    start_col = panel_start[0]
    panel_parts = []
    for panel_index in range(PANEL_T):
        column_id = start_col + panel_index
        column = lax.dynamic_index_in_dim(assembled, column_id // cols_grid, axis=1, keepdims=False)
        panel_parts.append(spread_2(column, "col", column_id % cols_grid))
    row_panel = jnp.concatenate(panel_parts, axis=2)
    col_panel = spread_2(every_other(row_panel, parent_cols, offset), "row", root_row)
    scaled = jnp.einsum(
        "axp,pq->axq",
        row_panel,
        pivot_inverse,
        precision=highest,
        preferred_element_type=jnp.float32,
    )
    trailing = jnp.einsum(
        "axq,byq->abxy", scaled, col_panel, precision=highest, preferred_element_type=jnp.float32
    )
    big_rows = jnp.arange(parent_rows, dtype=jnp.int32) * rows_grid + my_row
    big_cols = jnp.arange(parent_cols, dtype=jnp.int32) * cols_grid + my_col
    window = (big_rows[:, None] >= big_cols[None, :]) & (big_cols[None, :] >= start_col + PANEL_T)
    result = jnp.where(window[:, :, None, None], assembled - trailing, assembled)
    return result[:, None, :, None]


def solution(mesh):
    placed = (
        P(None, "row", None, "col", None, None),
        P(None, "row", None, "col", None, None),
        P(None, "row", None, None),
        P(None, "row", None, "col"),
        P(),
        P(),
        P(),
        P(),
    )
    return jax.shard_map(
        per_device,
        mesh=mesh,
        in_specs=placed,
        out_specs=P(None, "row", None, "col", None, None),
        check_vma=False,
    )
```

profile of v0, /device:TPU:0, one launch (start us, length us, event | category | flops | bytes accessed | tf_op | source)
XLA Modules:
  0.0 810.4 jit_solution(2350074608308215927)
XLA Ops:
  7.3 29.4 %all-gather.2.cloned.1.call-done = f32[8,8,64,128]{3,2,1,0:T(8,128)} async-done(((f32[8,1,64,128]{3,2,1,0:T(8,128)}), f32[8,8,64,128]{3,2,1,0:T(8,128)}) %all-gather.2.cloned.1.call-update) | async-done | bytes 2097168 | tf_op jit(solution)/shard_map/all_gather | solution.py:66
  36.7 17.0 %convolution_bitcast_fusion = f32[16,4,8,64,64]{3,4,2,0,1:T(8,128)} fusion(f32[4,16,64,128,1]{3,2,4,1,0:T(8,128)} %bitcast.109, f32[8,1,64,128]{3,2,1,0:T(8,128)} %param.11), kind=kOutput, calls=%fused_computation.1 | convolution fusion | flops 3221225472 | bytes 10747904 | tf_op jit(solution)/shard_map/trp,scup->cstru/dot_general | solution.py:69
  53.7 17.6 %copy.33 = f32[16,4,8,64,64]{4,3,2,1,0:T(8,128)} copy(f32[16,4,8,64,64]{3,4,2,0,1:T(8,128)} %convolution_bitcast_fusion) | data formatting | bytes 16777216 | tf_op jit(solution)/shard_map/trp,scup->cstru/transpose | solution.py:69
  71.3 14.7 %reshape.468 = f32[64,8,4096]{2,1,0:T(8,128)} reshape(f32[16,4,8,64,64]{4,3,2,1,0:T(8,128)} %copy.33) | data formatting | bytes 16777216 | tf_op jit(solution)/shard_map/reshape | solution.py:77
  90.2 81.4 %reduce-scatter.2.cloned.1.call-done = f32[4,8,4096]{2,1,0:T(8,128)} async-done(((f32[64,8,4096]{2,1,0:T(8,128)}), f32[4,8,4096]{2,1,0:T(8,128)}) %reduce-scatter.2.cloned.1.call-update) | async-done | bytes 524304 | tf_op jit(solution)/shard_map/reduce_scatter | solution.py:76
  176.0 56.6 %all-reduce.5.cloned.1.call-done = f32[4,64,128]{2,1,0:T(8,128)} async-done(((f32[4,64,128]{2,1,0:T(8,128)}), f32[4,64,128]{2,1,0:T(8,128)}) %all-reduce.5.cloned.1.call-update) | async-done | bytes 131088 | tf_op jit(solution)/shard_map/psum | solution.py:12
  232.6 3.9 fusion.9
  237.0 26.3 %collective-permute-done = f32[8,4,128,128]{2,3,0,1:T(8,128)} collective-permute-done((f32[8,4,128,128]{2,3,0,1:T(8,128)S(1)}, f32[8,4,128,128]{2,3,0,1:T(8,128)}, u32[]{:S(2)}, u32[]{:S(2)}) %collective-permute-start) | collective-permute-done | bytes 2097184 | tf_op jit(solution)/shard_map/ppermute | solution.py:17
  265.3 45.3 %collective-permute-done.1 = f32[8,4,128,128]{2,3,0,1:T(8,128)S(1)} collective-permute-done((f32[8,4,128,128]{2,3,0,1:T(8,128)S(1)}, f32[8,4,128,128]{2,3,0,1:T(8,128)S(1)}, u32[]{:S(2)}, u32[]{:S(2)}) %collective-permute-start.1) | collective-permute-done | bytes 2097184 | tf_op jit(solution)/shard_map/ppermute | solution.py:17
  311.9 45.3 %collective-permute-done.2 = f32[8,4,128,128]{2,3,0,1:T(8,128)S(1)} collective-permute-done((f32[8,4,128,128]{2,3,0,1:T(8,128)S(1)}, f32[8,4,128,128]{2,3,0,1:T(8,128)S(1)}, u32[]{:S(2)}, u32[]{:S(2)}) %collective-permute-start.2) | collective-permute-done | bytes 2097184 | tf_op jit(solution)/shard_map/ppermute | solution.py:17
  359.7 47.1 %collective-permute-done.3 = f32[8,4,128,128]{2,3,0,1:T(8,128)S(1)} collective-permute-done((f32[8,4,128,128]{2,3,0,1:T(8,128)S(1)}, f32[8,4,128,128]{2,3,0,1:T(8,128)S(1)}, u32[]{:S(2)}, u32[]{:S(2)}) %collective-permute-start.3) | collective-permute-done | bytes 2097184 | tf_op jit(solution)/shard_map/ppermute | solution.py:17
  407.3 49.8 %collective-permute-done.4 = f32[8,4,128,128]{2,3,0,1:T(8,128)S(1)} collective-permute-done((f32[8,4,128,128]{2,3,0,1:T(8,128)S(1)}, f32[8,4,128,128]{2,3,0,1:T(8,128)S(1)}, u32[]{:S(2)}, u32[]{:S(2)}) %collective-permute-start.4) | collective-permute-done | bytes 2097184 | tf_op jit(solution)/shard_map/ppermute | solution.py:17
  457.6 65.4 %collective-permute-done.5 = f32[8,4,128,128]{2,3,0,1:T(8,128)S(1)} collective-permute-done((f32[8,4,128,128]{2,3,0,1:T(8,128)S(1)}, f32[8,4,128,128]{2,3,0,1:T(8,128)S(1)}, u32[]{:S(2)}, u32[]{:S(2)}) %collective-permute-start.5) | collective-permute-done | bytes 2097184 | tf_op jit(solution)/shard_map/ppermute | solution.py:17
  524.5 26.5 %collective-permute-done.6 = f32[8,4,128,128]{2,3,0,1:T(8,128)} collective-permute-done((f32[8,4,128,128]{2,3,0,1:T(8,128)S(1)}, f32[8,4,128,128]{2,3,0,1:T(8,128)}, u32[]{:S(2)}, u32[]{:S(2)}) %collective-permute-start.6) | collective-permute-done | bytes 2097184 | tf_op jit(solution)/shard_map/ppermute | solution.py:17
  551.0 3.2 broadcast_select_fusion.7
  558.2 13.0 %bitcast_add_fusion = f32[16,8,128,128]{3,1,2,0:T(8,128)S(1)} fusion(f32[16,1,8,1,128,128]{5,4,3,2,1,0:T(8,128)} %param.9, f32[16,4,128,128]{3,0,2,1:T(8,128)S(1)} %fusion.21, s32[4]{0:T(128)S(1)} %and_select_fusion), kind=kOutput, calls=%fused_computation.3 | convolution fusion | flops 102760480 | bytes 20971536 | tf_op jit(solution)/shard_map/bs,asxy->abxy/dot_general | solution.py:126
  572.4 5.8 broadcast_select_fusion
  581.1 104.7 %all-reduce.9.cloned.1.call-done = (f32[16,128,128]{2,1,0:T(8,128)}, f32[16,128,128]{2,1,0:T(8,128)}, f32[16,128,128]{2,1,0:T(8,128)}, f32[16,128,128]{2,1,0:T(8,128)}) async-done(((f32[16,128,128]{2,1,0:T(8,128)}, f32[16,128,128]{2,1,0:T(8,128)}, f32[16,128,128]{2,1,0:T(8,128)}, f32[16,128,128]{2,1,0:T(8,128)}), (f32[16,128,128]{2,1,0:T(8,128)}, f32[16,128,128]{2,1,0:T(8,128)}, f32[16,128,128]{2,1,0:T(8,128)}, ...) | async-done | bytes 4194320 | tf_op jit(solution)/shard_map/psum | solution.py:12
  692.5 9.9 %fusion.10 = f32[16,128,512]{2,1,0:T(8,128)} fusion(f32[16,128,512]{2,1,0:T(8,128)} %copy-done.2, f32[512,512]{1,0:T(8,128)S(1)} %copy-done), kind=kOutput, calls=%fused_computation.14 | convolution fusion | flops 6442450944 | bytes 9437184 | tf_op jit(solution)/shard_map/axp,pq->axq/dot_general | solution.py:138
  702.4 55.5 %all-reduce.7.cloned.1.call-done = f32[8,128,512]{2,1,0:T(8,128)} async-done(((f32[8,128,512]{2,1,0:T(8,128)}), f32[8,128,512]{2,1,0:T(8,128)}) %all-reduce.7.cloned.1.call-update) | async-done | bytes 2097168 | tf_op jit(solution)/shard_map/psum | solution.py:12
  757.9 18.0 %fusion.1 = f32[8,128,16,128]{3,1,2,0:T(8,128)} fusion(f32[16,128,512]{2,1,0:T(8,128)} %fusion.10, f32[8,128,512]{2,1,0:T(8,128)} %all-reduce.7.cloned.1.call-done), kind=kOutput, calls=%fused_computation.4 | convolution fusion | flops 12884901888 | bytes 14680064 | tf_op jit(solution)/shard_map/axq,byq->abxy/dot_general | solution.py:145
  775.9 9.4 %copy.42 = f32[8,128,16,128]{1,0,3,2:T(8,128)} copy(f32[8,128,16,128]{3,1,2,0:T(8,128)} %fusion.1) | data formatting | bytes 16777216 | tf_op jit(solution)/shard_map/axq,byq->abxy/dot_general | solution.py:145
  785.3 10.2 %fusion = f32[16,1,8,1,128,128]{5,2,4,0,3,1:T(8,128)} fusion(f32[16,8,128,128]{3,1,2,0:T(8,128)} %copy-done.1, f32[8,128,16,128]{1,0,3,2:T(8,128)} %copy.42, pred[16,8]{1,0:T(8,128)(4,1)S(1)} %compare_and_fusion), kind=kLoop, calls=%fused_computation.2 | loop fusion | flops 4194304 | bytes 25165952 | tf_op jit(solution)/shard_map/broadcast_in_dim | solution.py:152
  795.4 8.2 %copy.43 = f32[16,1,8,1,128,128]{5,4,3,2,1,0:T(8,128)} copy(f32[16,1,8,1,128,128]{5,2,4,0,3,1:T(8,128)} %fusion) | data formatting | bytes 16777216 | tf_op jit(solution)/shard_map/broadcast_in_dim | solution.py:152
  (80 shorter events, 31.7 us)
Async XLA Ops:
  6.5 686.0 %copy-start = (f32[512,512]{1,0:T(8,128)S(1)}, f32[512,512]{1,0:T(8,128)}, u32[]{:S(2)}) copy-start(f32[512,512]{1,0:T(8,128)} %param.15) | copy-start | bytes 3145732
  6.5 30.2 %all-gather.2.cloned.1.call-start = ((), (), s32[]{:S(2)}) async-start(), calls=%async_computation.2 | async-start | bytes 2359296 | tf_op jit(solution)/shard_map/all_gather | solution.py:66
  7.3 164.4 %reduce-scatter.2.cloned.1.call-start = ((), (), s32[]{:S(2)}) async-start(), calls=%async_computation.3 | async-start | bytes 8912896 | tf_op jit(solution)/shard_map/reduce_scatter | solution.py:76
  86.1 0.9 copy-start.7
  86.1 1.8 copy-start.8
  86.1 2.3 copy-start.3
  86.1 146.5 %all-reduce.5.cloned.1.call-start = ((), (), s32[]{:S(2)}) async-start(), calls=%async_computation.1 | async-start | bytes 262144 | tf_op jit(solution)/shard_map/psum | solution.py:12
  87.7 598.1 %all-reduce.9.cloned.1.call-start = ((), (), s32[]{:S(2)}) async-start(), calls=%async_computation.5 | async-start | bytes 8388608 | tf_op jit(solution)/shard_map/psum | solution.py:12
  176.0 60.6 %copy-start.9 = (s32[64]{0:T(128)S(1)}, s32[64]{0:T(128)}, u32[]{:S(2)}) copy-start(s32[64]{0:T(128)} %param.13) | copy-start | bytes 772
  236.6 26.8 %collective-permute-start = (f32[8,4,128,128]{2,3,0,1:T(8,128)S(1)}, f32[8,4,128,128]{2,3,0,1:T(8,128)}, u32[]{:S(2)}, u32[]{:S(2)}) collective-permute-start(f32[8,4,128,128]{2,3,0,1:T(8,128)S(1)} %fusion.9), channel_id=1, source_target_pairs={{0,16},{16,32},{32,48},{48,64},{64,80},{80,96},{96,112},{112,0},{1... | collective-permute-start | bytes 6291464 | tf_op jit(solution)/shard_map/ppermute | solution.py:17
  265.3 45.4 %collective-permute-start.1 = (f32[8,4,128,128]{2,3,0,1:T(8,128)S(1)}, f32[8,4,128,128]{2,3,0,1:T(8,128)S(1)}, u32[]{:S(2)}, u32[]{:S(2)}) collective-permute-start(f32[8,4,128,128]{2,3,0,1:T(8,128)S(1)} %broadcast_select_fusion.1), channel_id=1, source_target_pairs={{0,32},{16,48},{32,64},{48,80},{64,96},{80,112},{96,0},{112,16},{1... | collective-permute-start | bytes 6291464 | tf_op jit(solution)/shard_map/ppermute | solution.py:17
  311.1 46.1 %collective-permute-start.2 = (f32[8,4,128,128]{2,3,0,1:T(8,128)S(1)}, f32[8,4,128,128]{2,3,0,1:T(8,128)S(1)}, u32[]{:S(2)}, u32[]{:S(2)}) collective-permute-start(f32[8,4,128,128]{2,3,0,1:T(8,128)S(1)} %broadcast_select_fusion.2), channel_id=1, source_target_pairs={{0,64},{16,80},{32,96},{48,112},{64,0},{80,16},{96,32},{112,48},{1... | collective-permute-start | bytes 6291464 | tf_op jit(solution)/shard_map/ppermute | solution.py:17
  357.6 49.2 %collective-permute-start.3 = (f32[8,4,128,128]{2,3,0,1:T(8,128)S(1)}, f32[8,4,128,128]{2,3,0,1:T(8,128)S(1)}, u32[]{:S(2)}, u32[]{:S(2)}) collective-permute-start(f32[8,4,128,128]{2,3,0,1:T(8,128)S(1)} %broadcast_select_fusion.3), channel_id=1, source_target_pairs={{0,1},{1,2},{2,3},{3,4},{4,5},{5,6},{6,7},{7,8},{8,9},{9,10},{10,1... | collective-permute-start | bytes 6291464 | tf_op jit(solution)/shard_map/ppermute | solution.py:17
  407.2 49.9 %collective-permute-start.4 = (f32[8,4,128,128]{2,3,0,1:T(8,128)S(1)}, f32[8,4,128,128]{2,3,0,1:T(8,128)S(1)}, u32[]{:S(2)}, u32[]{:S(2)}) collective-permute-start(f32[8,4,128,128]{2,3,0,1:T(8,128)S(1)} %broadcast_select_fusion.4), channel_id=1, source_target_pairs={{0,2},{1,3},{2,4},{3,5},{4,6},{5,7},{6,8},{7,9},{8,10},{9,11},{10,... | collective-permute-start | bytes 6291464 | tf_op jit(solution)/shard_map/ppermute | solution.py:17
  457.5 65.5 %collective-permute-start.5 = (f32[8,4,128,128]{2,3,0,1:T(8,128)S(1)}, f32[8,4,128,128]{2,3,0,1:T(8,128)S(1)}, u32[]{:S(2)}, u32[]{:S(2)}) collective-permute-start(f32[8,4,128,128]{2,3,0,1:T(8,128)S(1)} %broadcast_select_fusion.5), channel_id=1, source_target_pairs={{0,4},{1,5},{2,6},{3,7},{4,8},{5,9},{6,10},{7,11},{8,12},{9,13},{1... | collective-permute-start | bytes 6291464 | tf_op jit(solution)/shard_map/ppermute | solution.py:17
  523.3 27.7 %collective-permute-start.6 = (f32[8,4,128,128]{2,3,0,1:T(8,128)S(1)}, f32[8,4,128,128]{2,3,0,1:T(8,128)}, u32[]{:S(2)}, u32[]{:S(2)}) collective-permute-start(f32[8,4,128,128]{2,3,0,1:T(8,128)S(1)} %broadcast_select_fusion.6), channel_id=1, source_target_pairs={{0,8},{1,9},{2,10},{3,11},{4,12},{5,13},{6,14},{7,15},{8,0},{9,1},... | collective-permute-start | bytes 6291464 | tf_op jit(solution)/shard_map/ppermute | solution.py:17
  571.2 7.0 copy-start.1
  580.9 177.0 %all-reduce.7.cloned.1.call-start = ((), (), s32[]{:S(2)}) async-start(), calls=%async_computation.4 | async-start | bytes 4194304 | tf_op jit(solution)/shard_map/psum | solution.py:12
  685.8 1.5 copy-start.6
  685.8 1.9 copy-start.5
  687.4 1.3 copy-start.4
  688.8 2.0 copy-start.2
Sparse Core Ops, SparseCore 0:
  9.1 27.6 all-gather.1
  86.2 85.3 reduce-scatter.1
  174.0 58.6 all-reduce.4
  581.0 104.7 all-reduce.8
  692.5 65.3 all-reduce.6
where the time goes:
time: 820 us; the launch traced here: 810 us
  waiting for transfers between devices  634 us (77%)
  matrix products  66.6 us (8%)
  local copies, waits for them, and re-layouts  62.5 us (8%)
  other arithmetic  29.3 us (4%)
  between operations  14.4 us (2%)
    ppermute x7, waiting for transfers between devices, from_behind(): return lax.ppermute(x, axis, [(i, (i + by) % count) for i in range(count)])  306 us
    psum x3, waiting for transfers between devices, spread_2(): return lax.psum(jnp.where(mine, x, jnp.zeros_like(x)), axis)  217 us
    reduce_scatter x1, waiting for transfers between devices, per_device(): lax.psum_scatter(products.reshape(lax.axis_size('col') * local_cols, loca...  81.4 us
    all_gather x1, waiting for transfers between devices, per_device(): all_pivots = lax.all_gather(pivot_basis, 'row', axis=1, tiled=True)  29.4 us
    dot_general x1, matrix products, per_device(): jnp.einsum('axq,byq->abxy', scaled, col_panel, precision=highest, preferr...  18 us
    transpose x1, local copies, waits for them, and re-layouts, per_device(): jnp.einsum('trp,scup->cstru', own_pivots, grouped, precision=highest, pre...  17.6 us
    dot_general x1, matrix products, per_device(): jnp.einsum('trp,scup->cstru', own_pivots, grouped, precision=highest, pre...  17 us
  transfers between devices with their start and end apart: 12, of which 12 were waited for; matrix products, arithmetic and copies ran while one was open for 2% of the time, Pallas kernels for 0%

commit v1 on v0

--- a/solution.py
+++ b/solution.py
@@ -5,6 +5,24 @@
 
 PANEL_T = 4
 highest = lax.Precision.HIGHEST
+
+
+def gather_around(value, axis, dim):
+    ways, here, step = (lax.axis_size(axis), lax.axis_index(axis), value.shape[dim])
+    dims = [n * ways if d == dim else n for d, n in enumerate(value.shape)]
+    full = lax.dynamic_update_slice_in_dim(
+        jnp.zeros(dims, value.dtype), value, here * step, axis=dim
+    )
+    going_up = going_down = value
+    for far in range(1, ways // 2 + 1):
+        going_up = lax.ppermute(going_up, axis, [(d, (d + 1) % ways) for d in range(ways)])
+        full = lax.dynamic_update_slice_in_dim(full, going_up, (here - far) % ways * step, axis=dim)
+        if 2 * far < ways:
+            going_down = lax.ppermute(going_down, axis, [(d, (d - 1) % ways) for d in range(ways)])
+            full = lax.dynamic_update_slice_in_dim(
+                full, going_down, (here + far) % ways * step, axis=dim
+            )
+    return full
 
 
 def spread_2(x, axis, root):
@@ -63,7 +81,7 @@
     own_pivots = pivot_basis[:, 0]
     basis_picked = every_other(row_basis[:, 0], local_cols, offset)
     col_basis = spread_2(basis_picked, "row", root_row)
-    all_pivots = lax.all_gather(pivot_basis, "row", axis=1, tiled=True)
+    all_pivots = gather_around(pivot_basis, "row", 1)
     pivot_width = pivot_basis.shape[3]
     grouped = all_pivots.reshape(local_cols, cols_grid, rank_max, pivot_width)
     products = jnp.einsum(

time: 820 us -> 756 us (0.922)
  waiting for transfers between devices: 634 us -> 555 us
  starting transfers between devices: 3.56 us -> 13.8 us
    psum x3, waiting for transfers between devices: 217 us -> 159 us  [spread_2(): return lax.psum(jnp.where(mine, x, jnp.zeros_like(x)), axis)]
    all_gather x1 -> x0, waiting for transfers between devices: 29.4 us -> none  [per_device(): all_pivots = lax.all_gather(pivot_basis, 'row', axis=1, tiled=True)]
    ppermute x0 -> x7, waiting for transfers between devices: none -> 15.6 us  [the longest x4 14.7 us: gather_around(): lax.ppermute(going_up, axis, [(d, (d + 1) % ways) for d in range(ways)])]
    ppermute x0 -> x7, starting transfers between devices: none -> 8.88 us  [the longest x3 8.87 us: gather_around(): lax.ppermute(going_down, axis, [(d, (d - 1) % ways) for d in range(ways)])]
  transfers between devices with their start and end apart: 12 -> 18, of which waited for: 12 -> 15; matrix products, arithmetic and copies ran while one was open for 2% -> 3% of each run, Pallas kernels for 0% -> 0%
where the time goes in v1:
time: 756 us; the launch traced here: 747 us
  waiting for transfers between devices  555 us (73%)
  local copies, waits for them, and re-layouts  66.8 us (9%)
  matrix products  65.4 us (9%)
  other arithmetic  29.4 us (4%)
  between operations  16.4 us (2%)
  starting transfers between devices  13.8 us (2%)
    ppermute x7, waiting for transfers between devices, from_behind(): return lax.ppermute(x, axis, [(i, (i + by) % count) for i in range(count)])  299 us
    psum x3, waiting for transfers between devices, spread_2(): return lax.psum(jnp.where(mine, x, jnp.zeros_like(x)), axis)  159 us
    reduce_scatter x1, waiting for transfers between devices, per_device(): lax.psum_scatter(products.reshape(lax.axis_size('col') * local_cols, loca...  80.8 us
    dot_general x1, matrix products, per_device(): jnp.einsum('axq,byq->abxy', scaled, col_panel, precision=highest, preferr...  18 us
    transpose x1, local copies, waits for them, and re-layouts, per_device(): jnp.einsum('trp,scup->cstru', own_pivots, grouped, precision=highest, pre...  17.7 us
    dot_general x1, matrix products, per_device(): jnp.einsum('trp,scup->cstru', own_pivots, grouped, precision=highest, pre...  15.8 us
  transfers between devices with their start and end apart: 18, of which 15 were waited for; matrix products, arithmetic and copies ran while one was open for 3% of the time, Pallas kernels for 0%

profile of v1, /device:TPU:0, one launch (start us, length us, event | category | flops | bytes accessed | tf_op | source)
XLA Modules:
  0.0 746.7 jit_solution(4988780816553582456)
XLA Ops:
  10.3 4.4 collective-permute-done
  18.1 4.0 collective-permute-done.2
  31.2 5.1 collective-permute-done.6
  36.3 15.8 %convolution_bitcast_fusion = f32[16,4,8,64,64]{3,4,2,0,1:T(8,128)} fusion(f32[4,16,64,128,1]{3,2,4,1,0:T(8,128)S(1)} %bitcast.104, f32[8,1,64,128]{3,2,1,0:T(8,128)S(1)} %copy-done.4), kind=kOutput, calls=%fused_computation.1 | convolution fusion | flops 3221225472 | bytes 10747904 | tf_op jit(solution)/shard_map/trp,scup->cstru/dot_general | solution.py:87
  52.1 17.7 %copy.33 = f32[16,4,8,64,64]{4,3,2,1,0:T(8,128)} copy(f32[16,4,8,64,64]{3,4,2,0,1:T(8,128)} %convolution_bitcast_fusion) | data formatting | bytes 16777216 | tf_op jit(solution)/shard_map/trp,scup->cstru/transpose | solution.py:87
  69.7 14.7 %reshape.468 = f32[64,8,4096]{2,1,0:T(8,128)} reshape(f32[16,4,8,64,64]{4,3,2,1,0:T(8,128)} %copy.33) | data formatting | bytes 16777216 | tf_op jit(solution)/shard_map/reshape | solution.py:95
  88.6 80.8 %reduce-scatter.2.cloned.1.call-done = f32[4,8,4096]{2,1,0:T(8,128)} async-done(((f32[64,8,4096]{2,1,0:T(8,128)}), f32[4,8,4096]{2,1,0:T(8,128)}) %reduce-scatter.2.cloned.1.call-update) | async-done | bytes 524304 | tf_op jit(solution)/shard_map/reduce_scatter | solution.py:94
  173.8 3.9 fusion.9
  178.2 26.3 %collective-permute-done.7 = f32[8,4,128,128]{2,3,0,1:T(8,128)} collective-permute-done((f32[8,4,128,128]{2,3,0,1:T(8,128)S(1)}, f32[8,4,128,128]{2,3,0,1:T(8,128)}, u32[]{:S(2)}, u32[]{:S(2)}) %collective-permute-start.7) | collective-permute-done | bytes 2097184 | tf_op jit(solution)/shard_map/ppermute | solution.py:35
  206.8 46.3 %collective-permute-done.8 = f32[8,4,128,128]{2,3,0,1:T(8,128)S(1)} collective-permute-done((f32[8,4,128,128]{2,3,0,1:T(8,128)S(1)}, f32[8,4,128,128]{2,3,0,1:T(8,128)S(1)}, u32[]{:S(2)}, u32[]{:S(2)}) %collective-permute-start.8) | collective-permute-done | bytes 2097184 | tf_op jit(solution)/shard_map/ppermute | solution.py:35
  255.5 44.5 %collective-permute-done.9 = f32[8,4,128,128]{2,3,0,1:T(8,128)S(1)} collective-permute-done((f32[8,4,128,128]{2,3,0,1:T(8,128)S(1)}, f32[8,4,128,128]{2,3,0,1:T(8,128)S(1)}, u32[]{:S(2)}, u32[]{:S(2)}) %collective-permute-start.9) | collective-permute-done | bytes 2097184 | tf_op jit(solution)/shard_map/ppermute | solution.py:35
  301.9 46.2 %collective-permute-done.10 = f32[8,4,128,128]{2,3,0,1:T(8,128)S(1)} collective-permute-done((f32[8,4,128,128]{2,3,0,1:T(8,128)S(1)}, f32[8,4,128,128]{2,3,0,1:T(8,128)S(1)}, u32[]{:S(2)}, u32[]{:S(2)}) %collective-permute-start.10) | collective-permute-done | bytes 2097184 | tf_op jit(solution)/shard_map/ppermute | solution.py:35
  348.6 49.8 %collective-permute-done.11 = f32[8,4,128,128]{2,3,0,1:T(8,128)S(1)} collective-permute-done((f32[8,4,128,128]{2,3,0,1:T(8,128)S(1)}, f32[8,4,128,128]{2,3,0,1:T(8,128)S(1)}, u32[]{:S(2)}, u32[]{:S(2)}) %collective-permute-start.11) | collective-permute-done | bytes 2097184 | tf_op jit(solution)/shard_map/ppermute | solution.py:35
  399.3 59.6 %collective-permute-done.12 = f32[8,4,128,128]{2,3,0,1:T(8,128)S(1)} collective-permute-done((f32[8,4,128,128]{2,3,0,1:T(8,128)S(1)}, f32[8,4,128,128]{2,3,0,1:T(8,128)S(1)}, u32[]{:S(2)}, u32[]{:S(2)}) %collective-permute-start.12) | collective-permute-done | bytes 2097184 | tf_op jit(solution)/shard_map/ppermute | solution.py:35
  460.6 26.5 %collective-permute-done.13 = f32[8,4,128,128]{2,3,0,1:T(8,128)} collective-permute-done((f32[8,4,128,128]{2,3,0,1:T(8,128)S(1)}, f32[8,4,128,128]{2,3,0,1:T(8,128)}, u32[]{:S(2)}, u32[]{:S(2)}) %collective-permute-start.13) | collective-permute-done | bytes 2097184 | tf_op jit(solution)/shard_map/ppermute | solution.py:35
  494.2 13.0 %bitcast_add_fusion = f32[16,8,128,128]{3,1,2,0:T(8,128)S(1)} fusion(f32[16,1,8,1,128,128]{5,4,3,2,1,0:T(8,128)} %param.9, f32[16,4,128,128]{3,0,2,1:T(8,128)S(1)} %fusion.21, s32[4]{0:T(128)S(1)} %and_select_fusion), kind=kOutput, calls=%fused_computation.3 | convolution fusion | flops 102760480 | bytes 20971536 | tf_op jit(solution)/shard_map/bs,asxy->abxy/dot_general | solution.py:144
  508.5 5.8 broadcast_select_fusion
  517.2 104.2 %all-reduce.9.cloned.1.call-done = (f32[16,128,128]{2,1,0:T(8,128)}, f32[16,128,128]{2,1,0:T(8,128)}, f32[16,128,128]{2,1,0:T(8,128)}, f32[16,128,128]{2,1,0:T(8,128)}) async-done(((f32[16,128,128]{2,1,0:T(8,128)}, f32[16,128,128]{2,1,0:T(8,128)}, f32[16,128,128]{2,1,0:T(8,128)}, f32[16,128,128]{2,1,0:T(8,128)}), (f32[16,128,128]{2,1,0:T(8,128)}, f32[16,128,128]{2,1,0:T(8,128)}, f32[16,128,128]{2,1,0:T(8,128)}, ...) | async-done | bytes 4194320 | tf_op jit(solution)/shard_map/psum | solution.py:30
  628.1 9.9 %fusion.10 = f32[16,128,512]{2,1,0:T(8,128)} fusion(f32[16,128,512]{2,1,0:T(8,128)} %copy-done.2, f32[512,512]{1,0:T(8,128)S(1)} %copy-done), kind=kOutput, calls=%fused_computation.14 | convolution fusion | flops 6442450944 | bytes 9437184 | tf_op jit(solution)/shard_map/axp,pq->axq/dot_general | solution.py:156
  638.0 55.2 %all-reduce.7.cloned.1.call-done = f32[8,128,512]{2,1,0:T(8,128)} async-done(((f32[8,128,512]{2,1,0:T(8,128)}), f32[8,128,512]{2,1,0:T(8,128)}) %all-reduce.7.cloned.1.call-update) | async-done | bytes 2097168 | tf_op jit(solution)/shard_map/psum | solution.py:30
  693.1 18.0 %fusion.1 = f32[8,128,16,128]{3,1,2,0:T(8,128)} fusion(f32[16,128,512]{2,1,0:T(8,128)} %fusion.10, f32[8,128,512]{2,1,0:T(8,128)} %all-reduce.7.cloned.1.call-done), kind=kOutput, calls=%fused_computation.4 | convolution fusion | flops 12884901888 | bytes 14680064 | tf_op jit(solution)/shard_map/axq,byq->abxy/dot_general | solution.py:163
  711.2 9.4 %copy.42 = f32[8,128,16,128]{1,0,3,2:T(8,128)} copy(f32[8,128,16,128]{3,1,2,0:T(8,128)} %fusion.1) | data formatting | bytes 16777216 | tf_op jit(solution)/shard_map/axq,byq->abxy/dot_general | solution.py:163
  720.6 10.2 %fusion = f32[16,1,8,1,128,128]{5,2,4,0,3,1:T(8,128)} fusion(f32[16,8,128,128]{3,1,2,0:T(8,128)} %copy-done.1, f32[8,128,16,128]{1,0,3,2:T(8,128)} %copy.42, pred[16,8]{1,0:T(8,128)(4,1)S(1)} %compare_and_fusion), kind=kLoop, calls=%fused_computation.2 | loop fusion | flops 4194304 | bytes 25165952 | tf_op jit(solution)/shard_map/broadcast_in_dim | solution.py:170
  730.8 8.2 %copy.43 = f32[16,1,8,1,128,128]{5,4,3,2,1,0:T(8,128)} copy(f32[16,1,8,1,128,128]{5,2,4,0,3,1:T(8,128)} %fusion) | data formatting | bytes 16777216 | tf_op jit(solution)/shard_map/broadcast_in_dim | solution.py:170
  (102 shorter events, 51.0 us)
Async XLA Ops:
  7.4 620.7 %copy-start = (f32[512,512]{1,0:T(8,128)S(1)}, f32[512,512]{1,0:T(8,128)}, u32[]{:S(2)}) copy-start(f32[512,512]{1,0:T(8,128)} %param.15) | copy-start | bytes 3145732
  7.4 10.5 %copy-start.4 = (f32[8,1,64,128]{3,2,1,0:T(8,128)S(1)}, f32[8,1,64,128]{3,2,1,0:T(8,128)}, u32[]{:S(2)}) copy-start(f32[8,1,64,128]{3,2,1,0:T(8,128)} %param.11) | copy-start | bytes 786436
  7.4 162.1 %reduce-scatter.2.cloned.1.call-start = ((), (), s32[]{:S(2)}) async-start(), calls=%async_computation.2 | async-start | bytes 8912896 | tf_op jit(solution)/shard_map/reduce_scatter | solution.py:94
  7.4 7.3 collective-permute-start
  7.4 7.3 collective-permute-start.1
  14.7 7.3 collective-permute-start.2
  14.7 9.3 %collective-permute-start.3 = (f32[8,1,64,128]{3,2,1,0:T(8,128)}, f32[8,1,64,128]{3,2,1,0:T(8,128)}, u32[]{:S(2)}, u32[]{:S(2)}) collective-permute-start(f32[8,1,64,128]{3,2,1,0:T(8,128)} %collective-permute-done.1), channel_id=1, source_target_pairs={{0,112},{16,0},{32,16},{48,32},{64,48},{80,64},{96,80},{112,96},{1... | collective-permute-start | bytes 786440 | tf_op jit(solution)/shard_map/ppermute | solution.py:21
  22.0 7.2 collective-permute-start.4
  24.0 7.2 collective-permute-start.5
  29.2 7.0 collective-permute-start.6
  84.5 2.3 copy-start.3
  84.5 89.3 %all-reduce.5.cloned.1.call-start = ((), (), s32[]{:S(2)}) async-start(), calls=%async_computation.1 | async-start | bytes 262144 | tf_op jit(solution)/shard_map/psum | solution.py:30
  86.1 535.3 %all-reduce.9.cloned.1.call-start = ((), (), s32[]{:S(2)}) async-start(), calls=%async_computation.4 | async-start | bytes 8388608 | tf_op jit(solution)/shard_map/psum | solution.py:30
  173.8 4.0 copy-start.10
  177.7 26.8 %collective-permute-start.7 = (f32[8,4,128,128]{2,3,0,1:T(8,128)S(1)}, f32[8,4,128,128]{2,3,0,1:T(8,128)}, u32[]{:S(2)}, u32[]{:S(2)}) collective-permute-start(f32[8,4,128,128]{2,3,0,1:T(8,128)S(1)} %fusion.9), channel_id=1, source_target_pairs={{0,16},{16,32},{32,48},{48,64},{64,80},{80,96},{96,112},{112,0},{1... | collective-permute-start | bytes 6291464 | tf_op jit(solution)/shard_map/ppermute | solution.py:35
  206.4 46.6 %collective-permute-start.8 = (f32[8,4,128,128]{2,3,0,1:T(8,128)S(1)}, f32[8,4,128,128]{2,3,0,1:T(8,128)S(1)}, u32[]{:S(2)}, u32[]{:S(2)}) collective-permute-start(f32[8,4,128,128]{2,3,0,1:T(8,128)S(1)} %broadcast_select_fusion.1), channel_id=1, source_target_pairs={{0,32},{16,48},{32,64},{48,80},{64,96},{80,112},{96,0},{112,16},{1... | collective-permute-start | bytes 6291464 | tf_op jit(solution)/shard_map/ppermute | solution.py:35
  253.5 46.5 %collective-permute-start.9 = (f32[8,4,128,128]{2,3,0,1:T(8,128)S(1)}, f32[8,4,128,128]{2,3,0,1:T(8,128)S(1)}, u32[]{:S(2)}, u32[]{:S(2)}) collective-permute-start(f32[8,4,128,128]{2,3,0,1:T(8,128)S(1)} %broadcast_select_fusion.2), channel_id=1, source_target_pairs={{0,64},{16,80},{32,96},{48,112},{64,0},{80,16},{96,32},{112,48},{1... | collective-permute-start | bytes 6291464 | tf_op jit(solution)/shard_map/ppermute | solution.py:35
  300.4 47.7 %collective-permute-start.10 = (f32[8,4,128,128]{2,3,0,1:T(8,128)S(1)}, f32[8,4,128,128]{2,3,0,1:T(8,128)S(1)}, u32[]{:S(2)}, u32[]{:S(2)}) collective-permute-start(f32[8,4,128,128]{2,3,0,1:T(8,128)S(1)} %broadcast_select_fusion.3), channel_id=1, source_target_pairs={{0,1},{1,2},{2,3},{3,4},{4,5},{5,6},{6,7},{7,8},{8,9},{9,10},{10,1... | collective-permute-start | bytes 6291464 | tf_op jit(solution)/shard_map/ppermute | solution.py:35
  348.5 49.9 %collective-permute-start.11 = (f32[8,4,128,128]{2,3,0,1:T(8,128)S(1)}, f32[8,4,128,128]{2,3,0,1:T(8,128)S(1)}, u32[]{:S(2)}, u32[]{:S(2)}) collective-permute-start(f32[8,4,128,128]{2,3,0,1:T(8,128)S(1)} %broadcast_select_fusion.4), channel_id=1, source_target_pairs={{0,2},{1,3},{2,4},{3,5},{4,6},{5,7},{6,8},{7,9},{8,10},{9,11},{10,... | collective-permute-start | bytes 6291464 | tf_op jit(solution)/shard_map/ppermute | solution.py:35
  398.9 60.1 %collective-permute-start.12 = (f32[8,4,128,128]{2,3,0,1:T(8,128)S(1)}, f32[8,4,128,128]{2,3,0,1:T(8,128)S(1)}, u32[]{:S(2)}, u32[]{:S(2)}) collective-permute-start(f32[8,4,128,128]{2,3,0,1:T(8,128)S(1)} %broadcast_select_fusion.5), channel_id=1, source_target_pairs={{0,4},{1,5},{2,6},{3,7},{4,8},{5,9},{6,10},{7,11},{8,12},{9,13},{1... | collective-permute-start | bytes 6291464 | tf_op jit(solution)/shard_map/ppermute | solution.py:35
  459.3 27.7 %collective-permute-start.13 = (f32[8,4,128,128]{2,3,0,1:T(8,128)S(1)}, f32[8,4,128,128]{2,3,0,1:T(8,128)}, u32[]{:S(2)}, u32[]{:S(2)}) collective-permute-start(f32[8,4,128,128]{2,3,0,1:T(8,128)S(1)} %broadcast_select_fusion.6), channel_id=1, source_target_pairs={{0,8},{1,9},{2,10},{3,11},{4,12},{5,13},{6,14},{7,15},{8,0},{9,1},... | collective-permute-start | bytes 6291464 | tf_op jit(solution)/shard_map/ppermute | solution.py:35
  507.2 7.1 copy-start.1
  517.0 176.2 %all-reduce.7.cloned.1.call-start = ((), (), s32[]{:S(2)}) async-start(), calls=%async_computation.3 | async-start | bytes 4194304 | tf_op jit(solution)/shard_map/psum | solution.py:30
  624.4 2.0 copy-start.2
  (5 other events, 7.4 us)
Sparse Core Ops, SparseCore 0:
  84.6 84.7 reduce-scatter.1
  517.1 104.2 all-reduce.8
Sparse Core Ops, SparseCore 1:
  87.3 60.4 all-reduce.4
  628.1 65.0 all-reduce.6
